TPU v7x, 32 devices: a whole 2x2x4 slice. The times are simulated.
32 devices in a mesh: grp: 4 (over y, x), col: 8 (over z, core).
Axes of the slice: x: 2, y: 2, z: 4, core: 2. Of those that a mesh axis runs over, the one named last changes fastest.
Arguments:
- right_side: float32 [2048, 2048], P('grp', 'col'), may hold values from -6 to 6
- solved_factor: float32 [2048, 6144], P('grp', 'col'), may hold values from -0.078125 to 0.078125
- solved_users: float32 [6144, 2048], P('col'), may hold values from -6 to 6
- diag_inverse: float32 [2048, 512], P('grp'), may hold values from -0.25 to 0.25
- coupling: float32 [2048, 1536], P('grp'), may hold values from -0.25 to 0.25
Outputs:
- solution: float32 [2048, 2048], P('grp', 'col')
All inputs are finite; a program needn't handle non-finite values.
Results may differ from a plain program's by a relative error of at most 0.0001.
Values sent between devices are 32-bit elements; how exact they have to be, the bound alone decides.
A program may use at most 64 MiB of HBM per device.

v0:
```python
import functools

import jax
import jax.numpy as jnp
from jax import lax
from jax.experimental import pallas as pl
from jax.experimental.pallas import tpu as pltpu
from jax.sharding import PartitionSpec as P

highest = lax.Precision.HIGHEST
MESH = pl.DeviceIdType.MESH
LANES = 128


def broadcast(block, axis, source):
    block = jnp.where(lax.axis_index(axis) == source, block, jnp.zeros_like(block))
    return lax.psum(block, axis)


def apply_plain(matrix, vector):
    return jnp.dot(matrix, vector, precision=highest, preferred_element_type=jnp.float32)


def run_chain(residue, diag_inverse, coupling, apply_left):
    groups = lax.axis_size("grp")
    position = lax.axis_index("grp")
    block_rows = diag_inverse.shape[0]
    result = jnp.zeros_like(residue)
    for section_index in range(groups):
        candidate = apply_left(diag_inverse, residue)
        result = jnp.where(position == section_index, candidate, result)
        if section_index + 1 < groups:
            solved = broadcast(candidate, "grp", section_index)
            coupling_block = coupling[
                :, section_index * block_rows : (section_index + 1) * block_rows
            ]
            residue = jnp.where(
                position > section_index, residue - apply_left(coupling_block, solved), residue
            )
    return result


def by_collectives(right_side, solved_factor, solved_users, diag_inverse, coupling):
    partials = jnp.dot(
        solved_factor, solved_users, precision=highest, preferred_element_type=jnp.float32
    )
    shares = lax.psum_scatter(partials, "col", scatter_dimension=1, tiled=True)
    residue = right_side - shares
    return run_chain(residue, diag_inverse, coupling, apply_plain)


def halves(x):
    high = x.astype(jnp.bfloat16)
    return high, (x - high.astype(jnp.float32)).astype(jnp.bfloat16)


def left_form(x):
    high, low = halves(x)
    return jnp.concatenate([high, high, low], axis=1)


def right_form(x):
    high, low = halves(x)
    return jnp.concatenate([high, low, high], axis=0)


def dot(a, b):
    return jnp.dot(a, b, preferred_element_type=jnp.float32)


def swap(x):
    return pltpu.roll(x, LANES // 2, 1)


def first_lanes(shape):
    return lax.broadcasted_iota(jnp.int32, shape, 1) < LANES // 2


def pack(x):
    upper, lower = x[: x.shape[0] // 2], x[x.shape[0] // 2 :]
    return jnp.where(first_lanes(upper.shape), upper, swap(lower))


def unpack(x):
    return jnp.concatenate([x, swap(x)], axis=0)


def kernel(
    groups, chips, pieces,
    rhs_hbm, factor_hbm, users_hbm, diag_hbm, coupling_hbm,
    out_ref,
    rhs, factor, users, diag, coupling,
    factor3, diag3, effect3,
    own, give, take, from_low, from_high, total, spare, work, solved, arrived,
    load_sem, users_sem, give_sem, take_sem, hop_sem, low_sem, high_sem,
    spare_sem, total_sem, solved_sem, arrived_sem,
):
    g = lax.axis_index("grp")
    c = lax.axis_index("col")
    z = c // 2
    e = c % 2
    rows = rhs.shape[0]
    half = rows // 2
    width = rhs.shape[1]
    partner = (g, z * 2 + (1 - e))
    above = (g, c + 2)
    below = (g, c - 2)

    def block_of(b):
        j = b % chips
        return (b // chips) * chips + jnp.where(2 * z < chips, chips - 1 - j, j)

    loads = []
    for part in range(2):
        source = pl.multiple_of((e if part == 0 else 1 - e) * half, half)
        loads.append(pltpu.make_async_copy(
            factor_hbm.at[pl.ds(source, half)], factor.at[pl.ds(part * half, half)],
            load_sem.at[part]))
    later = [
        pltpu.make_async_copy(diag_hbm, diag, load_sem.at[2]),
        pltpu.make_async_copy(coupling_hbm, coupling, load_sem.at[3]),
        pltpu.make_async_copy(rhs_hbm, rhs, load_sem.at[4]),
    ]

    def users_load(b):
        i = block_of(b)
        column = pl.multiple_of(((i % chips) * 2 + i // chips) * width, width)
        return pltpu.make_async_copy(
            users_hbm.at[:, pl.ds(column, width)], users.at[b], users_sem.at[b])

    for copy in loads:
        copy.start()

    @pl.loop(0, 2 * chips)
    def _(b):
        users_load(b).start()

    out_ref[...] = jnp.zeros_like(out_ref)
    barrier = pltpu.get_barrier_semaphore()
    pl.semaphore_signal(barrier, inc=1, device_id=partner, device_id_type=MESH)
    for step in range(1, groups):
        pl.semaphore_signal(
            barrier, inc=1, device_id=((g + step) % groups, c), device_id_type=MESH)

    @pl.when(z > 0)
    def _():
        pl.semaphore_signal(barrier, inc=1, device_id=below, device_id_type=MESH)

    @pl.when(z < chips - 1)
    def _():
        pl.semaphore_signal(barrier, inc=1, device_id=above, device_id_type=MESH)

    for copy in loads:
        copy.wait()
    factor3[...] = left_form(factor[...])

    pl.semaphore_wait(
        barrier, groups + jnp.where(z > 0, 1, 0) + jnp.where(z < chips - 1, 1, 0))

    def give_copy(i, q):
        return pltpu.make_async_remote_copy(
            src_ref=give.at[i, q], dst_ref=take.at[i, q], send_sem=give_sem.at[i, q],
            recv_sem=take_sem.at[i, q], device_id=partner, device_id_type=MESH)

    def up(i, q):
        return pltpu.make_async_remote_copy(
            src_ref=own.at[i, q], dst_ref=from_low.at[i, q], send_sem=hop_sem.at[i, q],
            recv_sem=low_sem.at[i, q], device_id=above, device_id_type=MESH)

    def down(i, q):
        return pltpu.make_async_remote_copy(
            src_ref=own.at[i, q], dst_ref=from_high.at[i, q], send_sem=hop_sem.at[i, q],
            recv_sem=high_sem.at[i, q], device_id=below, device_id_type=MESH)

    def send_first(i, q):
        d = i % chips

        @pl.when(jnp.logical_and(z == 0, d > 0))
        def _():
            up(i, q).start()

        if chips > 1:
            @pl.when(jnp.logical_and(z == chips - 1, d < chips - 1))
            def _():
                down(i, q).start()

    def merge(b):
        i = block_of(b)
        for q in range(pieces):
            give_copy(i, q).wait()
            own[i, q] = own[i, q] + take[i, q]
            if q == 0:
                send_first(i, 0)

    @pl.loop(0, 2 * chips)
    def _(b):
        users_load(b).wait()
        i = block_of(b)
        product = dot(factor3[...], right_form(users[b]))
        for k in range(pieces // 2):
            tile = product[:, k * LANES : (k + 1) * LANES]
            turned = swap(tile)
            own[i, 2 * k] = pack(tile[:half])
            own[i, 2 * k + 1] = pack(turned[:half])
            give[i, 2 * k] = pack(tile[half:])
            give[i, 2 * k + 1] = pack(turned[half:])
        for q in range(pieces):
            give_copy(i, q).start()

        @pl.when(b > 0)
        def _():
            merge(b - 1)

    merge(2 * chips - 1)
    for q in range(1, pieces):
        @pl.loop(0, 2 * chips)
        def _(b):
            send_first(block_of(b), q)

    for copy in later:
        copy.start()

    def effect(h):
        @pl.loop(0, rows // (2 * LANES))
        def _(n):
            columns = pl.multiple_of(n * 2 * LANES, 2 * LANES)
            source = pl.multiple_of(h * rows + columns, 2 * LANES)
            product = dot(diag3[...], right_form(coupling[:, pl.ds(source, 2 * LANES)]))
            high, low = halves(product)
            effect3[h, :, pl.ds(columns, 2 * LANES)] = high
            effect3[h, :, pl.ds(rows + columns, 2 * LANES)] = high
            effect3[h, :, pl.ds(2 * rows + columns, 2 * LANES)] = low

    def total_copy(side, q):
        return pltpu.make_async_remote_copy(
            src_ref=spare.at[q], dst_ref=total.at[q, e],
            send_sem=spare_sem.at[q], recv_sem=total_sem.at[q],
            device_id=partner, device_id_type=MESH)

    def relay_up(q, side):
        for s in range(chips - 1):
            i = side * chips + chips - 1 - s

            @pl.when(jnp.logical_and(z > 0, chips - 1 - s > z))
            def _():
                up(i, q).wait_recv()
                own[i, q] = own[i, q] + from_low[i, q]
                up(i, q).start()

    def relay_down(q, side):
        for s in range(chips - 1):
            i = side * chips + s

            @pl.when(jnp.logical_and(z < chips - 1, s < z))
            def _():
                down(i, q).wait_recv()
                own[i, q] = own[i, q] + from_high[i, q]
                down(i, q).start()

    lower = 2 * z < chips

    def relay_near(p):
        @pl.when(lower)
        def _():
            relay_up(p // 2, p % 2)

        @pl.when(jnp.logical_not(lower))
        def _():
            relay_down(p // 2, p % 2)

    def finish_piece(p):
        q = p // 2
        side = p % 2

        @pl.when(lower)
        def _():
            relay_down(q, side)

        @pl.when(jnp.logical_not(lower))
        def _():
            relay_up(q, side)

        mine = side * chips + z

        @pl.when(z > 0)
        def _():
            up(mine, q).wait_recv()
            own[mine, q] = own[mine, q] + from_low[mine, q]

        @pl.when(z < chips - 1)
        def _():
            down(mine, q).wait_recv()
            own[mine, q] = own[mine, q] + from_high[mine, q]

        @pl.when(side == e)
        def _():
            total[q, e] = own[mine, q]

        @pl.when(side != e)
        def _():
            spare[q] = own[mine, q]
            total_copy(side, q).start()

    def solved_copy(source, target, q):
        return pltpu.make_async_remote_copy(
            src_ref=solved.at[q], dst_ref=arrived.at[source, q],
            send_sem=solved_sem.at[target, q], recv_sem=arrived_sem.at[source, q],
            device_id=(target, c), device_id_type=MESH)

    def solve_piece(q):
        columns = pl.ds(pl.multiple_of((q // 2) * LANES, LANES), LANES)
        odd = q % 2 == 1
        right = rhs[:, columns]
        right = jnp.where(odd, swap(right), right)
        total_copy(e, q).wait_recv()
        reduced = right - jnp.concatenate([unpack(total[q, 0]), unpack(total[q, 1])], axis=0)
        work[...] = dot(diag3[...], right_form(reduced))
        for h in range(groups - 1):
            @pl.when(h < g)
            def _():
                solved_copy(h, 0, q).wait_recv()
                work[...] = work[...] - dot(effect3[h], right_form(unpack(arrived[h, q])))
        result = work[...]

        @pl.when(g < groups - 1)
        def _():
            solved[q] = pack(result)
        for target in range(1, groups):
            @pl.when(target > g)
            def _():
                solved_copy(g, target, q).start()
        placed = jnp.where(odd, swap(result), result)
        mine = first_lanes(placed.shape) != odd
        out_ref[:, columns] = jnp.where(mine, placed, out_ref[:, columns])

    count = 2 * pieces

    relay_near(0)

    @pl.loop(0, count + groups - 1)
    def _(t):
        @pl.when(t + 1 < count)
        def _():
            relay_near(t + 1)

        @pl.when(t < count)
        def _():
            finish_piece(t)

        @pl.when(t == 0)
        def _():
            for copy in later:
                copy.wait()
            diag3[...] = left_form(diag[...])

        p = t - g

        @pl.when(jnp.logical_and(jnp.logical_and(p >= 0, p < count), (p + 2 * groups) % 2 == e))
        def _():
            solve_piece(p // 2)

        @pl.when(jnp.logical_and(t < groups - 1, t < g))
        def _():
            effect(t)

    @pl.loop(0, 2 * chips)
    def _(i):
        @pl.when(i % chips != z)
        def _():
            for q in range(pieces):
                pltpu.make_async_remote_copy(
                    src_ref=own.at[i, q], dst_ref=from_low.at[i, q], send_sem=hop_sem.at[i, q],
                    recv_sem=low_sem.at[i, q], device_id=partner, device_id_type=MESH
                ).wait_send()

    for q in range(pieces):
        total_copy(0, q).wait_send()
        for target in range(1, groups):
            @pl.when(target > g)
            def _():
                solved_copy(g, target, q).wait_send()


def by_kernel(right_side, solved_factor, solved_users, diag_inverse, coupling):
    groups = lax.axis_size("grp")
    chips = lax.axis_size("col") // 2
    rows, width = right_side.shape
    depth = solved_factor.shape[1]
    half = rows // 2
    pieces = width // (LANES // 2)
    f32, bf16 = jnp.float32, jnp.bfloat16
    unit = (half // 2, LANES)
    blocks = 2 * chips
    dma = pltpu.SemaphoreType.DMA
    scratch = [
        pltpu.VMEM((rows, width), f32),
        pltpu.VMEM((rows, depth), f32),
        pltpu.VMEM((blocks, depth, width), f32),
        pltpu.VMEM((rows, rows), f32),
        pltpu.VMEM(coupling.shape, f32),
        pltpu.VMEM((rows, 3 * depth), bf16),
        pltpu.VMEM((rows, 3 * rows), bf16),
        pltpu.VMEM((groups - 1, rows, 3 * rows), bf16),
        pltpu.VMEM((blocks, pieces) + unit, f32),
        pltpu.VMEM((blocks, pieces) + unit, f32),
        pltpu.VMEM((blocks, pieces) + unit, f32),
        pltpu.VMEM((blocks, pieces) + unit, f32),
        pltpu.VMEM((blocks, pieces) + unit, f32),
        pltpu.VMEM((pieces, 2) + unit, f32),
        pltpu.VMEM((pieces,) + unit, f32),
        pltpu.VMEM((rows, LANES), f32),
        pltpu.VMEM((pieces, half, LANES), f32),
        pltpu.VMEM((groups - 1, pieces, half, LANES), f32),
        dma((5,)), dma((blocks,)), dma((blocks, pieces)), dma((blocks, pieces)),
        dma((blocks, pieces)), dma((blocks, pieces)), dma((blocks, pieces)),
        dma((pieces,)), dma((pieces,)), dma((groups, pieces)), dma((groups, pieces)),
    ]
    return pl.pallas_call(
        functools.partial(kernel, groups, chips, pieces),
        out_shape=pltpu.VMEM((rows, width), f32),
        in_specs=[pl.BlockSpec(memory_space=pl.ANY)] * 5,
        out_specs=pl.BlockSpec(memory_space=pltpu.VMEM),
        scratch_shapes=scratch,
        compiler_params=pltpu.CompilerParams(
            collective_id=0, has_side_effects=True, vmem_limit_bytes=63 << 20),
    )(right_side, solved_factor, solved_users, diag_inverse, coupling)


def on_device(right_side, *others):
    whole_tiles = right_side.shape[1] % LANES == 0 and lax.axis_size("col") % 2 == 0
    return (by_kernel if whole_tiles else by_collectives)(right_side, *others)


def solution(mesh):
    placed = (P("grp", "col"), P("grp", "col"), P("col", None), P("grp", None), P("grp", None))
    return jax.shard_map(
        on_device, mesh=mesh, in_specs=placed, out_specs=P("grp", "col"), check_vma=False
    )
```

profile of v0, /device:TPU:7, one launch (start us, length us, event | category | flops | bytes accessed | tf_op | source)
XLA Modules:
  0.0 62.5 jit_solution(6125405132821020289)
XLA Ops:
  0.0 61.7 %shard_map.55 = f32[512,256]{1,0:T(8,128)S(1)} custom-call(f32[512,256]{1,0:T(8,128)} %rhs_hbm.1, f32[512,768]{1,0:T(8,128)} %factor_hbm.1, f32[768,2048]{1,0:T(8,128)} %users_hbm.1, f32[512,512]{1,0:T(8,128)} %diag_hbm.1, f32[512,1536]{1,0:T(8,128)} %coupling_hbm.1), custom_call_target="tpu_custom_call" | custom-call | tf_op jit(solution)/shard_map/pallas_call | solution.py:418
  61.7 0.8 %copy.7 = f32[512,256]{1,0:T(8,128)} copy(f32[512,256]{1,0:T(8,128)S(1)} %shard_map.55) | data formatting | bytes 1048576
where the time goes:
time: 62.6 us; the launch traced here: 62.5 us
  Pallas kernels  61.7 us (99%)
  local copies, waits for them, and re-layouts  0.8 us (1%)
    pallas_call x1, Pallas kernels, by_kernel(): pl.pallas_call(functools.partial(kernel, groups, chips, pieces), out_shap...  61.7 us

commit v1 on v0

v1 whole, which is shorter than its diff:
```python
import functools

import jax
import jax.numpy as jnp
from jax import lax
from jax.experimental import pallas as pl
from jax.experimental.pallas import tpu as pltpu
from jax.sharding import PartitionSpec as P

highest = lax.Precision.HIGHEST
MESH = pl.DeviceIdType.MESH
LANES = 128
PIECE = 32
LAG = 1
WAIT = 2
JOIN = 6


def broadcast(block, axis, source):
    block = jnp.where(lax.axis_index(axis) == source, block, jnp.zeros_like(block))
    return lax.psum(block, axis)


def apply_plain(matrix, vector):
    return jnp.dot(matrix, vector, precision=highest, preferred_element_type=jnp.float32)


def run_chain(residue, diag_inverse, coupling, apply_left):
    groups = lax.axis_size("grp")
    position = lax.axis_index("grp")
    block_rows = diag_inverse.shape[0]
    result = jnp.zeros_like(residue)
    for section_index in range(groups):
        candidate = apply_left(diag_inverse, residue)
        result = jnp.where(position == section_index, candidate, result)
        if section_index + 1 < groups:
            solved = broadcast(candidate, "grp", section_index)
            coupling_block = coupling[
                :, section_index * block_rows : (section_index + 1) * block_rows
            ]
            residue = jnp.where(
                position > section_index, residue - apply_left(coupling_block, solved), residue
            )
    return result


def by_collectives(right_side, solved_factor, solved_users, diag_inverse, coupling):
    partials = jnp.dot(
        solved_factor, solved_users, precision=highest, preferred_element_type=jnp.float32
    )
    shares = lax.psum_scatter(partials, "col", scatter_dimension=1, tiled=True)
    residue = right_side - shares
    return run_chain(residue, diag_inverse, coupling, apply_plain)


def halves(x):
    high = x.astype(jnp.bfloat16)
    return high, (x - high.astype(jnp.float32)).astype(jnp.bfloat16)


def left_form(x):
    high, low = halves(x)
    return jnp.concatenate([high, high, low], axis=1)


def right_form(x):
    high, low = halves(x)
    return jnp.concatenate([high, low, high], axis=0)


def dot(a, b):
    return jnp.dot(a, b, preferred_element_type=jnp.float32)


def apply_right(rows, matrix):
    count = rows.shape[0]
    high, low = halves(rows)
    both = dot(jnp.concatenate([high, low], axis=0), matrix[0])
    return both[:count] + both[count:] + dot(high, matrix[1])


def kernel(
    groups, chips, pieces, pairs,
    rhs_hbm, factor_hbm, users_hbm, diag_hbm, coupling_hbm,
    out_ref,
    rhs, factor, users, diag, coupling,
    factor3, diag3, rhs_t, diag_t, mix_t, mix, mix_in,
    own, give, take, from_low, from_high, ready, got, result,
    load_sem, users_sem, give_sem, take_sem, hop_sem, low_sem, high_sem,
    ready_sem, got_sem, mix_send_sem, mix_sem, pass_sem, passed_sem,
):
    g = lax.axis_index("grp")
    c = lax.axis_index("col")
    z = c // 2
    e = c % 2
    rows, width = rhs.shape
    half = rows // 2
    size = width // pieces
    last = chips - 1
    partner = (g, z * 2 + (1 - e))
    lower = 2 * z < chips

    barrier = pltpu.get_barrier_semaphore()
    pl.semaphore_signal(barrier, inc=1, device_id=partner, device_id_type=MESH)
    for step in range(1, groups):
        pl.semaphore_signal(
            barrier, inc=1, device_id=((g + step) % groups, c), device_id_type=MESH)

    @pl.when(z > 0)
    def _():
        pl.semaphore_signal(barrier, inc=1, device_id=(g, c - 2), device_id_type=MESH)

    @pl.when(z < last)
    def _():
        pl.semaphore_signal(barrier, inc=1, device_id=(g, c + 2), device_id_type=MESH)

    def chip_at(j):
        if j == last:
            return z
        high, low = last - j, j
        return jnp.where(
            lower, jnp.where(high <= z, high - 1, high), jnp.where(low >= z, low + 1, low))

    factor_load = pltpu.make_async_copy(factor_hbm, factor, load_sem.at[0])
    later = [
        pltpu.make_async_copy(diag_hbm, diag, load_sem.at[1]),
        pltpu.make_async_copy(coupling_hbm, coupling, load_sem.at[2]),
        pltpu.make_async_copy(rhs_hbm, rhs, load_sem.at[3]),
    ]

    def users_load(j, part):
        side = e if part else 1 - e
        column = pl.multiple_of((chip_at(j) * 2 + side) * width, width)
        return pltpu.make_async_copy(
            users_hbm.at[:, pl.ds(column, width)], users.at[2 * j + part],
            users_sem.at[2 * j + part])

    factor_load.start()
    for j in range(chips):
        for part in range(2):
            users_load(j, part).start()
    for copy in later:
        copy.start()

    def span(p):
        return pl.ds(pl.multiple_of(p * size, size), size)

    def give_copy(d, p):
        return pltpu.make_async_remote_copy(
            src_ref=give.at[d, span(p)], dst_ref=take.at[d, span(p)],
            send_sem=give_sem.at[d, p], recv_sem=take_sem.at[d, p],
            device_id=partner, device_id_type=MESH)

    def up(d, p):
        return pltpu.make_async_remote_copy(
            src_ref=own.at[d, span(p)], dst_ref=from_low.at[d, span(p)],
            send_sem=hop_sem.at[d, p], recv_sem=low_sem.at[d, p],
            device_id=(g, c + 2), device_id_type=MESH)

    def down(d, p):
        return pltpu.make_async_remote_copy(
            src_ref=own.at[d, span(p)], dst_ref=from_high.at[d, span(p)],
            send_sem=hop_sem.at[d, p], recv_sem=high_sem.at[d, p],
            device_id=(g, c - 2), device_id_type=MESH)

    def product(j, part):
        users_load(j, part).wait()
        block = dot(factor3[...], right_form(users[2 * j + part])).T
        (own if part else give)[chip_at(j)] = block

    def pair_up(d, at_once):
        @pl.loop(0, pieces)
        def _(p):
            give_copy(d, p).wait()
            own[d, span(p)] = own[d, span(p)] + take[d, span(p)]
            for r, i in at_once:
                @pl.when(p == i)
                def _():
                    launch(r, i)

    def launch(r, p):
        @pl.when(z == 0)
        def _():
            up(last - r, p).start()

        @pl.when(z == last)
        def _():
            down(r, p).start()

    def give_all(d):
        @pl.loop(0, pieces)
        def _(p):
            give_copy(d, p).start()

    def relay_up(r, p):
        d = last - r

        @pl.when(jnp.logical_and(z > 0, d > z))
        def _():
            up(d, p).wait_recv()
            own[d, span(p)] = own[d, span(p)] + from_low[d, span(p)]
            up(d, p).start()

    def relay_down(d, p):
        @pl.when(jnp.logical_and(z < last, d < z))
        def _():
            down(d, p).wait_recv()
            own[d, span(p)] = own[d, span(p)] + from_high[d, span(p)]
            down(d, p).start()

    def relay_near(q):
        for r in range(chips - 2):
            p = q - leads[r]

            @pl.when(jnp.logical_and(p >= 0, p < pieces))
            def _():
                @pl.when(lower)
                def _():
                    relay_up(r, p)

                @pl.when(jnp.logical_not(lower))
                def _():
                    relay_down(r, p)

    def relay_far(q):
        for r in range(chips // 2 - 1):
            p = q - leads[r]

            @pl.when(jnp.logical_and(p >= 0, p < pieces))
            def _():
                @pl.when(lower)
                def _():
                    relay_down(r, p)

                @pl.when(jnp.logical_not(lower))
                def _():
                    relay_up(r, p)

    def mix_copy(k, h, target):
        part = pl.ds(pl.multiple_of(e * half, half), half)
        i = pairs.index((k, h))
        return pltpu.make_async_remote_copy(
            src_ref=mix.at[h, part], dst_ref=mix_in.at[i, part],
            send_sem=mix_send_sem.at[i, target], recv_sem=mix_sem.at[i],
            device_id=(target, c), device_id_type=MESH)

    def mix_pass(k, h):
        part = pl.ds(pl.multiple_of(e * half, half), half)
        i = pairs.index((k, h))
        return pltpu.make_async_remote_copy(
            src_ref=mix_in.at[i, part], dst_ref=mix_in.at[i, part],
            send_sem=pass_sem.at[i], recv_sem=passed_sem.at[i],
            device_id=partner, device_id_type=MESH)

    def prepare():
        for copy in later:
            copy.wait()
        diag3[...] = left_form(diag[...])
        for h in range(groups - 1):
            @pl.when(h < g)
            def _():
                mix[h] = dot(diag3[...], right_form(coupling[:, h * rows : (h + 1) * rows]))
        for k, h in pairs:
            for target in range(k + 1, groups):
                @pl.when(g == k)
                def _():
                    mix_copy(k, h, target).start()

    def turn():
        rhs_t[...] = rhs[...].T
        high, low = halves(diag[...].T)
        diag_t[0] = high
        diag_t[1] = low

    def pass_mix():
        for k, h in pairs:
            @pl.when(g > k)
            def _():
                mix_copy(k, h, k + 1).wait_recv()
                mix_pass(k, h).start()

    def join_mix():
        for k, h in reversed(pairs):
            @pl.when(g > k)
            def _():
                mix_pass(k, h).wait()
                mix[h] = mix[h] - dot(left_form(mix[k]), right_form(mix_in[pairs.index((k, h))]))
        for h in range(groups - 1):
            @pl.when(h < g)
            def _():
                high, low = halves(mix[h].T)
                mix_t[h, 0] = high
                mix_t[h, 1] = low

    def ready_copy(source, buffer, target, p):
        return pltpu.make_async_remote_copy(
            src_ref=buffer.at[span(p)], dst_ref=got.at[source, span(p)],
            send_sem=ready_sem.at[target, p], recv_sem=got_sem.at[source, p],
            device_id=(target, c), device_id_type=MESH)

    def finish(p):
        @pl.when(z > 0)
        def _():
            up(z, p).wait_recv()
            own[z, span(p)] = own[z, span(p)] + from_low[z, span(p)]

        @pl.when(z < last)
        def _():
            down(z, p).wait_recv()
            own[z, span(p)] = own[z, span(p)] + from_high[z, span(p)]

        ready[span(p)] = apply_right(rhs_t[span(p)] - own[z, span(p)], diag_t)

        @pl.when(g < groups - 2)
        def _():
            for target in range(groups - 1, 0, -1):
                @pl.when(target > g)
                def _():
                    ready_copy(g, ready, target, p).start()

    def solve(p):
        result[span(p)] = ready[span(p)]
        for h in range(groups - 1):
            @pl.when(h < g)
            def _():
                ready_copy(h, ready, 0, p).wait_recv()
                result[span(p)] = result[span(p)] - apply_right(got[h, span(p)], mix_t.at[h])

        @pl.when(g == groups - 2)
        def _():
            ready_copy(g, result, groups - 1, p).start()

        per = LANES // size

        @pl.when(p % per == per - 1)
        def _():
            columns = pl.ds(pl.multiple_of((p // per) * LANES, LANES), LANES)
            out_ref[:, columns] = result[columns, :].T

    leads = [r + 1 if r else 0 for r in range(chips - 1)]
    order = [
        (r, q - leads[r]) for q in range(pieces + leads[-1]) for r in range(chips - 1)
        if 0 <= q - leads[r] < pieces]
    factor_load.wait()
    factor3[...] = left_form(factor[...])
    product(0, 0)
    product(0, 1)
    pl.semaphore_wait(
        barrier, groups + jnp.where(z > 0, 1, 0) + jnp.where(z < last, 1, 0))
    give_all(chip_at(0))
    for j in range(chips):
        if j + 1 < chips:
            product(j + 1, 0)
            give_all(chip_at(j + 1))
        open_now = []
        while order and order[0][0] <= j:
            open_now.append(order.pop(0))
        pair_up(chip_at(j), open_now if j == 0 else [])
        for r, p in open_now if j else []:
            launch(r, p)
        if j + 1 < chips:
            product(j + 1, 1)
        if j == chips - 2:
            prepare()

    turn()
    edge = jnp.logical_or(z == 0, z == last)
    behind = jnp.where(edge, chips // 2, leads[-1])
    extra = jnp.where(g == groups - 1, 2 * WAIT, WAIT)

    @pl.loop(0, pieces + leads[-1] + 2 * WAIT)
    def _(q):
        relay_near(q)
        p = q - behind

        @pl.when(jnp.logical_and(p >= 0, p < pieces))
        def _():
            finish(p)

        relay_far(q - LAG)

        @pl.when(q == JOIN - 1)
        def _():
            pass_mix()

        @pl.when(q == JOIN)
        def _():
            join_mix()

        p = q - behind - extra
        high = jnp.minimum(p + 1, pieces)
        low = jnp.where(q == JOIN, 0, jnp.maximum(p, 0))

        @pl.when(q >= JOIN)
        def _():
            @pl.loop(low, high)
            def _(i):
                solve(i)

    @pl.loop(0, chips)
    def _(d):
        @pl.when(d != z)
        def _():
            for p in range(pieces):
                pltpu.make_async_remote_copy(
                    src_ref=own.at[d, span(p)], dst_ref=from_low.at[d, span(p)],
                    send_sem=hop_sem.at[d, p], recv_sem=low_sem.at[d, p],
                    device_id=partner, device_id_type=MESH).wait_send()

    for target in range(1, groups):
        @pl.when(jnp.logical_and(target > g, jnp.logical_or(g < groups - 2, target == groups - 1)))
        def _():
            for p in range(pieces):
                ready_copy(g, ready, target, p).wait_send()
    for k, h in pairs:
        for target in range(k + 1, groups):
            @pl.when(g == k)
            def _():
                mix_copy(k, h, target).wait_send()


def by_kernel(right_side, solved_factor, solved_users, diag_inverse, coupling):
    groups = lax.axis_size("grp")
    chips = lax.axis_size("col") // 2
    rows, width = right_side.shape
    depth = solved_factor.shape[1]
    pieces = width // PIECE
    pairs = [(k, h) for k in range(1, groups - 2) for h in range(k)]
    f32, bf16 = jnp.float32, jnp.bfloat16
    dma = pltpu.SemaphoreType.DMA
    lines = pltpu.VMEM((chips, width, rows), f32)
    square = (rows, rows)
    scratch = [
        pltpu.VMEM((rows, width), f32),
        pltpu.VMEM((rows, depth), f32),
        pltpu.VMEM((2 * chips, depth, width), f32),
        pltpu.VMEM(square, f32),
        pltpu.VMEM(coupling.shape, f32),
        pltpu.VMEM((rows, 3 * depth), bf16),
        pltpu.VMEM((rows, 3 * rows), bf16),
        pltpu.VMEM((width, rows), f32),
        pltpu.VMEM((2,) + square, bf16),
        pltpu.VMEM((groups - 1, 2) + square, bf16),
        pltpu.VMEM((groups - 1,) + square, f32),
        pltpu.VMEM((max(len(pairs), 1),) + square, f32),
        lines, lines, lines, lines, lines,
        pltpu.VMEM((width, rows), f32),
        pltpu.VMEM((groups - 1, width, rows), f32),
        pltpu.VMEM((width, rows), f32),
        dma((4,)), dma((2 * chips,)), dma((chips, pieces)), dma((chips, pieces)),
        dma((chips, pieces)), dma((chips, pieces)), dma((chips, pieces)),
        dma((groups, pieces)), dma((groups, pieces)),
        dma((max(len(pairs), 1), groups)), dma((max(len(pairs), 1),)),
        dma((max(len(pairs), 1),)), dma((max(len(pairs), 1),)),
    ]
    return pl.pallas_call(
        functools.partial(kernel, groups, chips, pieces, pairs),
        out_shape=pltpu.VMEM((rows, width), f32),
        in_specs=[pl.BlockSpec(memory_space=pl.ANY)] * 5,
        out_specs=pl.BlockSpec(memory_space=pltpu.VMEM),
        scratch_shapes=scratch,
        compiler_params=pltpu.CompilerParams(
            collective_id=0, has_side_effects=True, vmem_limit_bytes=63 << 20),
    )(right_side, solved_factor, solved_users, diag_inverse, coupling)


def on_device(right_side, *others):
    whole_tiles = (
        right_side.shape[1] % LANES == 0 and right_side.shape[0] % LANES == 0
        and lax.axis_size("col") % 2 == 0 and lax.axis_size("col") > 4
        and lax.axis_size("grp") > 1)
    return (by_kernel if whole_tiles else by_collectives)(right_side, *others)


def solution(mesh):
    placed = (P("grp", "col"), P("grp", "col"), P("col", None), P("grp", None), P("grp", None))
    return jax.shard_map(
        on_device, mesh=mesh, in_specs=placed, out_specs=P("grp", "col"), check_vma=False
    )
```

time: 62.6 us -> 59.5 us (0.950)
  the two profiles are of different devices: /device:TPU:7 before, /device:TPU:14 now
where the time goes in v1:
time: 59.5 us; the launch traced here: 59.3 us
  Pallas kernels  58.5 us (98%)
  local copies, waits for them, and re-layouts  0.8 us (1%)
    pallas_call x1, Pallas kernels, by_kernel(): pl.pallas_call(functools.partial(kernel, groups, chips, pieces, pairs), o...  58.5 us

profile of v1, /device:TPU:14, one launch (start us, length us, event | category | flops | bytes accessed | tf_op | source)
XLA Modules:
  0.0 59.3 jit_solution(134330745442661500)
XLA Ops:
  0.0 58.5 %shard_map.55 = f32[512,256]{1,0:T(8,128)S(1)} custom-call(f32[512,256]{1,0:T(8,128)} %rhs_hbm.1, f32[512,768]{1,0:T(8,128)} %factor_hbm.1, f32[768,2048]{1,0:T(8,128)} %users_hbm.1, f32[512,512]{1,0:T(8,128)} %diag_hbm.1, f32[512,1536]{1,0:T(8,128)} %coupling_hbm.1), custom_call_target="tpu_custom_call" | custom-call | tf_op jit(solution)/shard_map/pallas_call | solution.py:456
  58.5 0.8 %copy.7 = f32[512,256]{1,0:T(8,128)} copy(f32[512,256]{1,0:T(8,128)S(1)} %shard_map.55) | data formatting | bytes 1048576

commit v2 on v1

--- a/solution.py
+++ b/solution.py
@@ -12,8 +12,10 @@
 LANES = 128
 PIECE = 32
 LAG = 1
-WAIT = 2
-JOIN = 6
+WAIT = 1
+PASS = 5
+JOIN = 7
+START = 8
 
 
 def broadcast(block, axis, source):
@@ -84,7 +86,7 @@
     rhs_hbm, factor_hbm, users_hbm, diag_hbm, coupling_hbm,
     out_ref,
     rhs, factor, users, diag, coupling,
-    factor3, diag3, rhs_t, diag_t, mix_t, mix, mix_in,
+    factor3, diag3, rhs_t, diag_t, mix_t, mix, blend, mix_in,
     own, give, take, from_low, from_high, ready, got, result,
     load_sem, users_sem, give_sem, take_sem, hop_sem, low_sem, high_sem,
     ready_sem, got_sem, mix_send_sem, mix_sem, pass_sem, passed_sem,
@@ -97,6 +99,7 @@
     half = rows // 2
     size = width // pieces
     last = chips - 1
+    per = LANES // size
     partner = (g, z * 2 + (1 - e))
     lower = 2 * z < chips
 
@@ -259,7 +262,9 @@
         for h in range(groups - 1):
             @pl.when(h < g)
             def _():
-                mix[h] = dot(diag3[...], right_form(coupling[:, h * rows : (h + 1) * rows]))
+                effect = dot(diag3[...], right_form(coupling[:, h * rows : (h + 1) * rows]))
+                mix[h] = effect
+                blend[h] = effect
         for k, h in pairs:
             for target in range(k + 1, groups):
                 @pl.when(g == k)
@@ -272,67 +277,68 @@
         diag_t[0] = high
         diag_t[1] = low
 
-    def pass_mix():
+    def pass_mix(step):
         for k, h in pairs:
-            @pl.when(g > k)
+            @pl.when(jnp.logical_and(g > k, step == k - 1))
             def _():
                 mix_copy(k, h, k + 1).wait_recv()
                 mix_pass(k, h).start()
 
-    def join_mix():
-        for k, h in reversed(pairs):
-            @pl.when(g > k)
-            def _():
-                mix_pass(k, h).wait()
-                mix[h] = mix[h] - dot(left_form(mix[k]), right_form(mix_in[pairs.index((k, h))]))
+    def join_mix(step):
+        for n, k in enumerate(range(groups - 2, 0, -1)):
+            @pl.when(jnp.logical_and(g > k, step == n))
+            def _():
+                for h in range(k):
+                    mix_pass(k, h).wait()
+                left = left_form(blend[k])
+                for h in range(k):
+                    right = right_form(mix_in[pairs.index((k, h))])
+                    blend[h] = blend[h] - dot(left, right)
+
+        @pl.when(step == max(groups - 3, 0))
+        def _():
+            for h in range(groups - 1):
+                @pl.when(h < g)
+                def _():
+                    high, low = halves(blend[h].T)
+                    mix_t[h, 0] = high
+                    mix_t[h, 1] = low
+
+    def ready_copy(source, target, p):
+        return pltpu.make_async_remote_copy(
+            src_ref=ready.at[span(p)], dst_ref=got.at[source, span(p)],
+            send_sem=ready_sem.at[target, p], recv_sem=got_sem.at[source, p],
+            device_id=(target, c), device_id_type=MESH)
+
+    def finish(p):
+        @pl.when(z > 0)
+        def _():
+            up(z, p).wait_recv()
+            own[z, span(p)] = own[z, span(p)] + from_low[z, span(p)]
+
+        @pl.when(z < last)
+        def _():
+            down(z, p).wait_recv()
+            own[z, span(p)] = own[z, span(p)] + from_high[z, span(p)]
+
+        ready[span(p)] = apply_right(rhs_t[span(p)] - own[z, span(p)], diag_t)
+
+        for target in range(groups - 1, 0, -1):
+            @pl.when(target > g)
+            def _():
+                ready_copy(g, target, p).start()
+
+    def solve(p, count):
+        these = pl.ds(pl.multiple_of(p * size, size), count * size)
+        result[these] = ready[these]
         for h in range(groups - 1):
             @pl.when(h < g)
             def _():
-                high, low = halves(mix[h].T)
-                mix_t[h, 0] = high
-                mix_t[h, 1] = low
-
-    def ready_copy(source, buffer, target, p):
-        return pltpu.make_async_remote_copy(
-            src_ref=buffer.at[span(p)], dst_ref=got.at[source, span(p)],
-            send_sem=ready_sem.at[target, p], recv_sem=got_sem.at[source, p],
-            device_id=(target, c), device_id_type=MESH)
-
-    def finish(p):
-        @pl.when(z > 0)
-        def _():
-            up(z, p).wait_recv()
-            own[z, span(p)] = own[z, span(p)] + from_low[z, span(p)]
-
-        @pl.when(z < last)
-        def _():
-            down(z, p).wait_recv()
-            own[z, span(p)] = own[z, span(p)] + from_high[z, span(p)]
-
-        ready[span(p)] = apply_right(rhs_t[span(p)] - own[z, span(p)], diag_t)
-
-        @pl.when(g < groups - 2)
-        def _():
-            for target in range(groups - 1, 0, -1):
-                @pl.when(target > g)
-                def _():
-                    ready_copy(g, ready, target, p).start()
-
-    def solve(p):
-        result[span(p)] = ready[span(p)]
-        for h in range(groups - 1):
-            @pl.when(h < g)
-            def _():
-                ready_copy(h, ready, 0, p).wait_recv()
-                result[span(p)] = result[span(p)] - apply_right(got[h, span(p)], mix_t.at[h])
-
-        @pl.when(g == groups - 2)
-        def _():
-            ready_copy(g, result, groups - 1, p).start()
-
-        per = LANES // size
-
-        @pl.when(p % per == per - 1)
+                for i in range(count):
+                    ready_copy(h, 0, p + i).wait_recv()
+                result[these] = result[these] - apply_right(got[h, these], mix_t.at[h])
+
+        @pl.when((p + count) % per == 0)
         def _():
             columns = pl.ds(pl.multiple_of((p // per) * LANES, LANES), LANES)
             out_ref[:, columns] = result[columns, :].T
@@ -344,31 +350,49 @@
     factor_load.wait()
     factor3[...] = left_form(factor[...])
     product(0, 0)
-    product(0, 1)
     pl.semaphore_wait(
         barrier, groups + jnp.where(z > 0, 1, 0) + jnp.where(z < last, 1, 0))
     give_all(chip_at(0))
+    product(0, 1)
+    sender = jnp.logical_and(g > 0, g < groups - 1)
+    edge = jnp.logical_or(z == 0, z == last)
     for j in range(chips):
-        if j + 1 < chips:
-            product(j + 1, 0)
-            give_all(chip_at(j + 1))
         open_now = []
         while order and order[0][0] <= j:
             open_now.append(order.pop(0))
-        pair_up(chip_at(j), open_now if j == 0 else [])
-        for r, p in open_now if j else []:
-            launch(r, p)
-        if j + 1 < chips:
-            product(j + 1, 1)
-        if j == chips - 2:
-            prepare()
+        if j == 0:
+            pair_up(chip_at(0), open_now)
+            product(1, 0)
+            give_all(chip_at(1))
+
+            @pl.when(jnp.logical_and(sender, jnp.logical_not(edge)))
+            def _():
+                prepare()
+
+            product(1, 1)
+        else:
+            if j + 1 < chips:
+                product(j + 1, 0)
+                give_all(chip_at(j + 1))
+            pair_up(chip_at(j), [])
+            for r, p in open_now:
+                launch(r, p)
+            if j == 1:
+                @pl.when(jnp.logical_and(sender, edge))
+                def _():
+                    prepare()
+
+            if j + 1 < chips:
+                product(j + 1, 1)
+
+    @pl.when(jnp.logical_not(sender))
+    def _():
+        prepare()
 
     turn()
-    edge = jnp.logical_or(z == 0, z == last)
     behind = jnp.where(edge, chips // 2, leads[-1])
-    extra = jnp.where(g == groups - 1, 2 * WAIT, WAIT)
-
-    @pl.loop(0, pieces + leads[-1] + 2 * WAIT)
+
+    @pl.loop(0, pieces + leads[-1] + WAIT)
     def _(q):
         relay_near(q)
         p = q - behind
@@ -379,23 +403,20 @@
 
         relay_far(q - LAG)
 
-        @pl.when(q == JOIN - 1)
-        def _():
-            pass_mix()
-
-        @pl.when(q == JOIN)
-        def _():
-            join_mix()
-
-        p = q - behind - extra
-        high = jnp.minimum(p + 1, pieces)
-        low = jnp.where(q == JOIN, 0, jnp.maximum(p, 0))
-
-        @pl.when(q >= JOIN)
-        def _():
-            @pl.loop(low, high)
+        pass_mix(q - PASS)
+
+        join_mix(q - JOIN)
+        p = q - behind - WAIT
+
+        @pl.when(q == START)
+        def _():
+            solve(0, per)
+
+        @pl.when(q >= START)
+        def _():
+            @pl.loop(jnp.where(q == START, per, jnp.maximum(p, per)), jnp.minimum(p + 1, pieces))
             def _(i):
-                solve(i)
+                solve(i, 1)
 
     @pl.loop(0, chips)
     def _(d):
@@ -408,10 +429,10 @@
                     device_id=partner, device_id_type=MESH).wait_send()
 
     for target in range(1, groups):
-        @pl.when(jnp.logical_and(target > g, jnp.logical_or(g < groups - 2, target == groups - 1)))
+        @pl.when(target > g)
         def _():
             for p in range(pieces):
-                ready_copy(g, ready, target, p).wait_send()
+                ready_copy(g, target, p).wait_send()
     for k, h in pairs:
         for target in range(k + 1, groups):
             @pl.when(g == k)
@@ -425,7 +446,7 @@
     rows, width = right_side.shape
     depth = solved_factor.shape[1]
     pieces = width // PIECE
-    pairs = [(k, h) for k in range(1, groups - 2) for h in range(k)]
+    pairs = [(k, h) for k in range(1, groups - 1) for h in range(k)]
     f32, bf16 = jnp.float32, jnp.bfloat16
     dma = pltpu.SemaphoreType.DMA
     lines = pltpu.VMEM((chips, width, rows), f32)
@@ -441,6 +462,7 @@
         pltpu.VMEM((width, rows), f32),
         pltpu.VMEM((2,) + square, bf16),
         pltpu.VMEM((groups - 1, 2) + square, bf16),
+        pltpu.VMEM((groups - 1,) + square, f32),
         pltpu.VMEM((groups - 1,) + square, f32),
         pltpu.VMEM((max(len(pairs), 1),) + square, f32),
         lines, lines, lines, lines, lines,

time: 59.5 us -> 54.2 us (0.911)
  Pallas kernels: 58.5 us -> 53.2 us
    pallas_call x1, Pallas kernels: 58.5 us -> 53.2 us  [by_kernel(): pl.pallas_call(functools.partial(kernel, groups, chips, pieces, pairs), o...]
where the time goes in v2:
time: 54.2 us; the launch traced here: 54 us
  Pallas kernels  53.2 us (98%)
  local copies, waits for them, and re-layouts  0.8 us (1%)
    pallas_call x1, Pallas kernels, by_kernel(): pl.pallas_call(functools.partial(kernel, groups, chips, pieces, pairs), o...  53.2 us

profile of v2, /device:TPU:14, one launch (start us, length us, event | category | flops | bytes accessed | tf_op | source)
XLA Modules:
  0.0 54.0 jit_solution(4793843600681517737)
XLA Ops:
  0.0 53.2 %shard_map.55 = f32[512,256]{1,0:T(8,128)S(1)} custom-call(f32[512,256]{1,0:T(8,128)} %rhs_hbm.1, f32[512,768]{1,0:T(8,128)} %factor_hbm.1, f32[768,2048]{1,0:T(8,128)} %users_hbm.1, f32[512,512]{1,0:T(8,128)} %diag_hbm.1, f32[512,1536]{1,0:T(8,128)} %coupling_hbm.1), custom_call_target="tpu_custom_call" | custom-call | tf_op jit(solution)/shard_map/pallas_call | solution.py:478
  53.2 0.8 %copy.7 = f32[512,256]{1,0:T(8,128)} copy(f32[512,256]{1,0:T(8,128)S(1)} %shard_map.55) | data formatting | bytes 1048576

commit v3 on v2

--- a/solution.py
+++ b/solution.py
@@ -14,8 +14,8 @@
 LAG = 1
 WAIT = 1
 PASS = 5
-JOIN = 7
-START = 8
+JOIN = 6
+START = 7
 
 
 def broadcast(block, axis, source):
@@ -255,16 +255,23 @@
             send_sem=pass_sem.at[i], recv_sem=passed_sem.at[i],
             device_id=partner, device_id_type=MESH)
 
+    def couple(h):
+        effect = dot(diag3[...], right_form(coupling[:, h * rows : (h + 1) * rows]))
+        mix[h] = effect
+        blend[h] = effect
+
+        @pl.when(g == h + 1)
+        def _():
+            high, low = halves(effect.T)
+            mix_t[h, 0] = high
+            mix_t[h, 1] = low
+
     def prepare():
-        for copy in later:
-            copy.wait()
         diag3[...] = left_form(diag[...])
-        for h in range(groups - 1):
+        for h in range(groups - 2):
             @pl.when(h < g)
             def _():
-                effect = dot(diag3[...], right_form(coupling[:, h * rows : (h + 1) * rows]))
-                mix[h] = effect
-                blend[h] = effect
+                couple(h)
         for k, h in pairs:
             for target in range(k + 1, groups):
                 @pl.when(g == k)
@@ -297,8 +304,8 @@
 
         @pl.when(step == max(groups - 3, 0))
         def _():
-            for h in range(groups - 1):
-                @pl.when(h < g)
+            for h in range(groups - 2):
+                @pl.when(h < g - 1)
                 def _():
                     high, low = halves(blend[h].T)
                     mix_t[h, 0] = high
@@ -348,8 +355,9 @@
         (r, q - leads[r]) for q in range(pieces + leads[-1]) for r in range(chips - 1)
         if 0 <= q - leads[r] < pieces]
     factor_load.wait()
+    users_load(0, 0).wait()
     factor3[...] = left_form(factor[...])
-    product(0, 0)
+    give[chip_at(0)] = dot(factor3[...], right_form(users[0])).T
     pl.semaphore_wait(
         barrier, groups + jnp.where(z > 0, 1, 0) + jnp.where(z < last, 1, 0))
     give_all(chip_at(0))
@@ -364,6 +372,8 @@
             pair_up(chip_at(0), open_now)
             product(1, 0)
             give_all(chip_at(1))
+            for copy in later:
+                copy.wait()
 
             @pl.when(jnp.logical_and(sender, jnp.logical_not(edge)))
             def _():
@@ -385,16 +395,25 @@
             if j + 1 < chips:
                 product(j + 1, 1)
 
-    @pl.when(jnp.logical_not(sender))
-    def _():
-        prepare()
-
-    turn()
     behind = jnp.where(edge, chips // 2, leads[-1])
 
     @pl.loop(0, pieces + leads[-1] + WAIT)
     def _(q):
+        @pl.when(q == 0)
+        def _():
+            turn()
+
         relay_near(q)
+
+        @pl.when(jnp.logical_and(q == 1, g == groups - 1))
+        def _():
+            diag3[...] = left_form(diag[...])
+
+        for h in range(groups - 1):
+            @pl.when(jnp.logical_and(q == h + 1, g == groups - 1))
+            def _():
+                couple(h)
+
         p = q - behind
 
         @pl.when(jnp.logical_and(p >= 0, p < pieces))

time: 54.2 us -> 52.6 us (0.970)
  Pallas kernels: 53.2 us -> 51.4 us
    pallas_call x1, Pallas kernels: 53.2 us -> 51.4 us  [by_kernel(): pl.pallas_call(functools.partial(kernel, groups, chips, pieces, pairs), o...]
where the time goes in v3:
time: 52.6 us; the launch traced here: 52.2 us
  Pallas kernels  51.4 us (98%)
  local copies, waits for them, and re-layouts  0.8 us (2%)
    pallas_call x1, Pallas kernels, by_kernel(): pl.pallas_call(functools.partial(kernel, groups, chips, pieces, pairs), o...  51.4 us

profile of v3, /device:TPU:14, one launch (start us, length us, event | category | flops | bytes accessed | tf_op | source)
XLA Modules:
  0.0 52.2 jit_solution(4805164782097463385)
XLA Ops:
  0.0 51.4 %shard_map.55 = f32[512,256]{1,0:T(8,128)S(1)} custom-call(f32[512,256]{1,0:T(8,128)} %rhs_hbm.1, f32[512,768]{1,0:T(8,128)} %factor_hbm.1, f32[768,2048]{1,0:T(8,128)} %users_hbm.1, f32[512,512]{1,0:T(8,128)} %diag_hbm.1, f32[512,1536]{1,0:T(8,128)} %coupling_hbm.1), custom_call_target="tpu_custom_call" | custom-call | tf_op jit(solution)/shard_map/pallas_call | solution.py:497
  51.4 0.8 %copy.7 = f32[512,256]{1,0:T(8,128)} copy(f32[512,256]{1,0:T(8,128)S(1)} %shard_map.55) | data formatting | bytes 1048576

commit v4 on v3

--- a/solution.py
+++ b/solution.py
@@ -16,6 +16,9 @@
 PASS = 5
 JOIN = 6
 START = 7
+EDGE_PASS = 5
+EDGE_JOIN = 6
+EDGE_START = 7
 
 
 def broadcast(block, axis, source):
@@ -139,11 +142,8 @@
             users_sem.at[2 * j + part])
 
     factor_load.start()
-    for j in range(chips):
-        for part in range(2):
-            users_load(j, part).start()
-    for copy in later:
-        copy.start()
+    for part in range(2):
+        users_load(0, part).start()
 
     def span(p):
         return pl.ds(pl.multiple_of(p * size, size), size)
@@ -356,6 +356,11 @@
         if 0 <= q - leads[r] < pieces]
     factor_load.wait()
     users_load(0, 0).wait()
+    for j in range(1, chips):
+        for part in range(2):
+            users_load(j, part).start()
+    for copy in later:
+        copy.start()
     factor3[...] = left_form(factor[...])
     give[chip_at(0)] = dot(factor3[...], right_form(users[0])).T
     pl.semaphore_wait(
@@ -396,6 +401,9 @@
                 product(j + 1, 1)
 
     behind = jnp.where(edge, chips // 2, leads[-1])
+    passing = jnp.where(edge, EDGE_PASS, PASS)
+    joining = jnp.where(edge, EDGE_JOIN, JOIN)
+    starting = jnp.where(edge, EDGE_START, START)
 
     @pl.loop(0, pieces + leads[-1] + WAIT)
     def _(q):
@@ -422,18 +430,18 @@
 
         relay_far(q - LAG)
 
-        pass_mix(q - PASS)
-
-        join_mix(q - JOIN)
+        pass_mix(q - passing)
+
+        join_mix(q - joining)
         p = q - behind - WAIT
 
-        @pl.when(q == START)
+        @pl.when(q == starting)
         def _():
             solve(0, per)
 
-        @pl.when(q >= START)
-        def _():
-            @pl.loop(jnp.where(q == START, per, jnp.maximum(p, per)), jnp.minimum(p + 1, pieces))
+        @pl.when(q >= starting)
+        def _():
+            @pl.loop(jnp.where(q == starting, per, jnp.maximum(p, per)), jnp.minimum(p + 1, pieces))
             def _(i):
                 solve(i, 1)
 

time: 52.6 us -> 51.9 us (0.987)
  Pallas kernels: 51.4 us -> 50.6 us
    pallas_call x1, Pallas kernels: 51.4 us -> 50.6 us  [by_kernel(): pl.pallas_call(functools.partial(kernel, groups, chips, pieces, pairs), o...]
where the time goes in v4:
time: 51.9 us; the launch traced here: 51.4 us
  Pallas kernels  50.6 us (97%)
  local copies, waits for them, and re-layouts  0.8 us (2%)
    pallas_call x1, Pallas kernels, by_kernel(): pl.pallas_call(functools.partial(kernel, groups, chips, pieces, pairs), o...  50.6 us

profile of v4, /device:TPU:14, one launch (start us, length us, event | category | flops | bytes accessed | tf_op | source)
XLA Modules:
  0.0 51.4 jit_solution(12085588671091498735)
XLA Ops:
  0.0 50.6 %shard_map.55 = f32[512,256]{1,0:T(8,128)S(1)} custom-call(f32[512,256]{1,0:T(8,128)} %rhs_hbm.1, f32[512,768]{1,0:T(8,128)} %factor_hbm.1, f32[768,2048]{1,0:T(8,128)} %users_hbm.1, f32[512,512]{1,0:T(8,128)} %diag_hbm.1, f32[512,1536]{1,0:T(8,128)} %coupling_hbm.1), custom_call_target="tpu_custom_call" | custom-call | tf_op jit(solution)/shard_map/pallas_call | solution.py:505
  50.6 0.8 %copy.7 = f32[512,256]{1,0:T(8,128)} copy(f32[512,256]{1,0:T(8,128)S(1)} %shard_map.55) | data formatting | bytes 1048576

commit v5 on v4

--- a/solution.py
+++ b/solution.py
@@ -272,11 +272,11 @@
             @pl.when(h < g)
             def _():
                 couple(h)
-        for k, h in pairs:
-            for target in range(k + 1, groups):
-                @pl.when(g == k)
-                def _():
-                    mix_copy(k, h, target).start()
+            for k in range(h + 1, groups - 1):
+                for target in range(k + 1, groups):
+                    @pl.when(g == k)
+                    def _():
+                        mix_copy(k, h, target).start()
 
     def turn():
         rhs_t[...] = rhs[...].T
@@ -338,12 +338,21 @@
     def solve(p, count):
         these = pl.ds(pl.multiple_of(p * size, size), count * size)
         result[these] = ready[these]
+
+        def subtract(h):
+            for i in range(count):
+                ready_copy(h, 0, p + i).wait_recv()
+            result[these] = result[these] - apply_right(got[h, these], mix_t.at[h])
+
+        for h in range(groups - 2, 0, -1):
+            @pl.when(g == groups - 1)
+            def _():
+                subtract(h)
+
         for h in range(groups - 1):
-            @pl.when(h < g)
-            def _():
-                for i in range(count):
-                    ready_copy(h, 0, p + i).wait_recv()
-                result[these] = result[these] - apply_right(got[h, these], mix_t.at[h])
+            @pl.when(jnp.logical_and(h < g, jnp.logical_or(h == 0, g < groups - 1)))
+            def _():
+                subtract(h)
 
         @pl.when((p + count) % per == 0)
         def _():
@@ -422,6 +431,7 @@
             def _():
                 couple(h)
 
+        pass_mix(q - passing)
         p = q - behind
 
         @pl.when(jnp.logical_and(p >= 0, p < pieces))
@@ -430,7 +440,6 @@
 
         relay_far(q - LAG)
 
-        pass_mix(q - passing)
 
         join_mix(q - joining)
         p = q - behind - WAIT

time: 51.9 us -> 51.7 us (level)
  no operation moved by 1% of the time
where the time goes in v5:
time: 51.7 us; the launch traced here: 51.6 us
  Pallas kernels  50.8 us (98%)
  local copies, waits for them, and re-layouts  0.8 us (2%)
    pallas_call x1, Pallas kernels, by_kernel(): pl.pallas_call(functools.partial(kernel, groups, chips, pieces, pairs), o...  50.8 us

profile of v5, /device:TPU:14, one launch (start us, length us, event | category | flops | bytes accessed | tf_op | source)
XLA Modules:
  0.0 51.6 jit_solution(9217087840312975594)
XLA Ops:
  0.0 50.8 %shard_map.55 = f32[512,256]{1,0:T(8,128)S(1)} custom-call(f32[512,256]{1,0:T(8,128)} %rhs_hbm.1, f32[512,768]{1,0:T(8,128)} %factor_hbm.1, f32[768,2048]{1,0:T(8,128)} %users_hbm.1, f32[512,512]{1,0:T(8,128)} %diag_hbm.1, f32[512,1536]{1,0:T(8,128)} %coupling_hbm.1), custom_call_target="tpu_custom_call" | custom-call | tf_op jit(solution)/shard_map/pallas_call | solution.py:514
  50.8 0.8 %copy.7 = f32[512,256]{1,0:T(8,128)} copy(f32[512,256]{1,0:T(8,128)S(1)} %shard_map.55) | data formatting | bytes 1048576
